TPU v7x, 512 devices: a whole 4x4x16 slice. The times are simulated.
512 devices in a mesh: dp: 16 (over x, z_lo), expert: 32 (over y, z_hi, core).
Axes of the slice: x: 4, y: 4, z: 16 (z_hi: 4, z_lo: 4; z = z_hi * 4 + z_lo), core: 2. Of those that a mesh axis runs over, the one named last changes fastest.
Arguments:
- tokens: bfloat16 [4096, 2560], P(('dp', 'expert')), may hold values from -24 to 24
- routes: int32 [4096, 6], P(('dp', 'expert')), may hold values from 0 to 7, all different within a row; in each aligned block of 8 rows (0 to 7, 8 to 15, ...) at most 7 rows name the same one
- router: float32 [2560, 8], replicated, may hold values from -0.125 to 0.125
- w_gate: bfloat16 [2560, 8192], P(None, 'expert'), may hold values from -0.125 to 0.125
- w_up: bfloat16 [2560, 8192], P(None, 'expert'), may hold values from -0.125 to 0.125
- w_down: bfloat16 [2560, 8192], P(None, 'expert'), may hold values from -0.1875 to 0.1875
- cotangent: bfloat16 [4096, 2560], P(('dp', 'expert')), may hold values from -6 to 6
Outputs:
- mixed: bfloat16 [4096, 2560], P(('dp', 'expert'))
- grad_tokens: bfloat16 [4096, 2560], P(('dp', 'expert'))
- grad_router: float32 [2560, 8], replicated
- grad_gate: float32 [2560, 8192], P('dp', 'expert')
- grad_up: float32 [2560, 8192], P('dp', 'expert')
- grad_down: float32 [2560, 8192], P('dp', 'expert')
Inputs may be any that keep to these rules, and one draw needn't show every extreme that they name: `routes`: each row names 6 different experts. Among the rows of one device no expert is named more than 7 times, and in every draw some expert is named exactly 7 times by the rows of some device.
All inputs are finite; a program needn't handle non-finite values.
Results may differ from a plain program's by a relative error of at most 0.02.
Values may be sent and summed in bfloat16 or wider, within the bound.
A program may use at most 64 MiB of HBM per device.

v0:
```python
import jax
import jax.numpy as jnp
from jax import lax
from jax.sharding import PartitionSpec as P


def expert_hidden(inputs, gate_matrix, up_matrix):
    gate_pre = jnp.dot(inputs, gate_matrix, preferred_element_type=jnp.float32)
    up_pre = jnp.dot(inputs, up_matrix, preferred_element_type=jnp.float32)
    hidden = (jax.nn.silu(gate_pre) * up_pre).astype(jnp.bfloat16)
    return (gate_pre, up_pre, hidden)


def expert_backward(slot_grad, gate_pre, up_pre, gate_matrix, up_matrix, down_matrix):
    hidden_grad = jnp.dot(slot_grad, down_matrix, preferred_element_type=jnp.float32)
    sigma = jax.nn.sigmoid(gate_pre)
    gate_grad = (hidden_grad * up_pre * sigma * (1.0 + gate_pre * (1.0 - sigma))).astype(
        jnp.bfloat16
    )
    up_grad = (hidden_grad * gate_pre * sigma).astype(jnp.bfloat16)
    contract = (((1,), (1,)), ((), ()))
    input_grad = lax.dot_general(
        gate_grad, gate_matrix, contract, preferred_element_type=jnp.float32
    )
    input_grad = input_grad + lax.dot_general(
        up_grad, up_matrix, contract, preferred_element_type=jnp.float32
    )
    return (gate_grad, up_grad, input_grad.astype(jnp.bfloat16))


def return_grads(input_part):
    return lax.all_to_all(input_part, "expert", split_axis=0, concat_axis=0, tiled=True)


def local(tokens, routes, router, w_gate, w_up, w_down, cotangent):
    features = tokens.shape[1]
    experts = router.shape[1]
    fanout = routes.shape[1]
    tok_count = tokens.shape[0]
    hidden_units = w_gate.shape[1]
    sharing = lax.axis_size("expert") // experts
    capacity = min(tok_count, 5 * fanout * tok_count // (4 * experts))
    highest = lax.Precision.HIGHEST
    tokens_wide = tokens.astype(jnp.float32)
    logits = jnp.dot(tokens_wide, router, precision=highest)
    expert_ids = jnp.arange(experts, dtype=jnp.int32)
    choose = routes[:, :, None] == expert_ids[None, None, :]
    choose_f = choose.astype(jnp.float32)
    picked = jnp.sum(choose_f * logits[:, None, :], axis=2)
    affinity = jax.nn.sigmoid(picked)
    denominator = jnp.sum(affinity, axis=1, keepdims=True)
    gate_values = affinity / denominator
    choose_i = choose.astype(jnp.int32)
    per_token = jnp.sum(choose_i, axis=1)
    before = jnp.cumsum(per_token, axis=0) - per_token
    position = jnp.sum(choose_i * before[:, None, :], axis=2)
    slot_ids = jnp.arange(capacity, dtype=jnp.int32)
    placed = choose_f[:, :, :, None] * (
        position[:, :, None, None] == slot_ids[None, None, None, :]
    ).astype(jnp.float32)
    slot_table = jnp.sum(placed, axis=1)
    gate_table = jnp.einsum("tkec,tk->tec", placed, gate_values)
    table_narrow = slot_table.astype(jnp.bfloat16)
    outgoing = jnp.einsum(
        "tec,td->ecd", table_narrow, tokens, preferred_element_type=jnp.float32
    ).astype(jnp.bfloat16)
    outgoing_all = jnp.repeat(outgoing, sharing, axis=0)

    def merge_parts(parts):
        wide_parts = parts.astype(jnp.float32)
        return jnp.sum(wide_parts.reshape(experts, sharing, capacity, features), axis=1)

    received = lax.all_to_all(outgoing_all, "expert", split_axis=0, concat_axis=0, tiled=True)
    sources, item_count, _ = received.shape
    expert_rows = received.reshape(sources * item_count, features)
    gate_pre, up_pre, hidden = expert_hidden(expert_rows, w_gate, w_up)
    output = lax.dot_general(
        hidden, w_down, (((1,), (1,)), ((), ())), preferred_element_type=jnp.float32
    )
    output = output.astype(jnp.bfloat16).reshape(sources, item_count, features)
    returned = lax.all_to_all(output, "expert", split_axis=0, concat_axis=0, tiled=True)
    returned, rows_kept, gate_kept, up_kept, hidden_kept = (
        returned,
        received,
        gate_pre.reshape(sources, item_count, hidden_units),
        up_pre.reshape(sources, item_count, hidden_units),
        hidden.reshape(sources, item_count, hidden_units),
    )
    expert_out = merge_parts(returned).astype(jnp.bfloat16)
    expert_wide = lax.optimization_barrier(expert_out).astype(jnp.float32)
    mixed = jnp.einsum("tec,ecd->td", gate_table, expert_wide).astype(jnp.bfloat16)
    grad_slots = jnp.einsum(
        "tec,td->ecd", table_narrow, cotangent, preferred_element_type=jnp.float32
    ).astype(jnp.bfloat16)
    slot_pull = jnp.sum(grad_slots.astype(jnp.float32) * expert_wide, axis=2)
    expert_pull = jnp.einsum("tec,ec->te", slot_table, slot_pull)
    gate_pull = jnp.sum(choose_f * expert_pull[:, None, :], axis=2)
    mean_pull = jnp.sum(gate_values * gate_pull, axis=1, keepdims=True)
    logit_grad = (gate_pull - mean_pull) / denominator * affinity * (1.0 - affinity)
    per_logit = jnp.sum(choose_f * logit_grad[:, :, None], axis=1)
    router_part = jnp.dot(tokens_wide.T, per_logit, precision=highest)
    grad_router = lax.psum(router_part, ("dp", "expert"))
    slot_gate = jnp.sum(gate_table, axis=0)
    grad_outgoing = (slot_gate[:, :, None] * grad_slots.astype(jnp.float32)).astype(jnp.bfloat16)
    grad_outgoing_all = jnp.repeat(grad_outgoing, sharing, axis=0)
    row_items = lax.all_to_all(outgoing_all, "expert", split_axis=0, concat_axis=0, tiled=True)
    grad_items = lax.all_to_all(
        grad_outgoing_all, "expert", split_axis=0, concat_axis=0, tiled=True
    )
    sources, item_count, _ = row_items.shape
    expert_rows = row_items.reshape(-1, features)
    grad_rows = grad_items.reshape(-1, features)
    gate_pre, up_pre, hidden = expert_hidden(expert_rows, w_gate, w_up)
    backward_gate_grad, backward_up_grad, input_part = expert_backward(
        grad_rows, gate_pre, up_pre, w_gate, w_up, w_down
    )
    input_back = return_grads(input_part.reshape(sources, item_count, features))
    input_back, rows_again, grads_again, hidden_again, gate_again, up_again = (
        input_back,
        row_items,
        grad_items,
        hidden.reshape(sources, item_count, hidden_units),
        backward_gate_grad.reshape(sources, item_count, hidden_units),
        backward_up_grad.reshape(sources, item_count, hidden_units),
    )
    rows_flat = rows_again.reshape(-1, features)
    grad_flat = grads_again.reshape(-1, features)
    hidden_flat = hidden_again.reshape(-1, hidden_units)
    gate_grad = gate_again.reshape(-1, hidden_units)
    up_grad = up_again.reshape(-1, hidden_units)
    contract = (((0,), (0,)), ((), ()))
    part_gate = lax.dot_general(rows_flat, gate_grad, contract, preferred_element_type=jnp.float32)
    part_up = lax.dot_general(rows_flat, up_grad, contract, preferred_element_type=jnp.float32)
    part_down = lax.dot_general(
        grad_flat, hidden_flat, contract, preferred_element_type=jnp.float32
    )
    summed = lax.psum_scatter(
        jnp.concatenate([part_gate, part_up, part_down], axis=1).astype(jnp.bfloat16),
        "dp",
        scatter_dimension=0,
        tiled=True,
    ).astype(jnp.float32)
    grad_gate = summed[:, :hidden_units]
    grad_up = summed[:, hidden_units : 2 * hidden_units]
    grad_down = summed[:, 2 * hidden_units :]
    input_grad = merge_parts(input_back).astype(jnp.bfloat16)
    input_wide = lax.optimization_barrier(input_grad).astype(jnp.float32)
    router_back = lax.dot_general(per_logit, router, (((1,), (1,)), ((), ())), precision=highest)
    grad_tokens = (jnp.einsum("tec,ecd->td", slot_table, input_wide) + router_back).astype(
        jnp.bfloat16
    )
    return (mixed, grad_tokens, grad_router, grad_gate, grad_up, grad_down)


def solution(mesh):
    return jax.shard_map(
        local,
        mesh=mesh,
        in_specs=(
            P(("dp", "expert"), None),
            P(("dp", "expert"), None),
            P(),
            P(None, "expert"),
            P(None, "expert"),
            P(None, "expert"),
            P(("dp", "expert"), None),
        ),
        out_specs=(
            P(("dp", "expert"), None),
            P(("dp", "expert"), None),
            P(),
            P("dp", "expert"),
            P("dp", "expert"),
            P("dp", "expert"),
        ),
        check_vma=False,
    )
```

profile of v0, /device:TPU:1, one launch (start us, length us, event | category | flops | bytes accessed | tf_op | source)
XLA Modules:
  0.0 811.4 jit_solution(12839090901430853241)
XLA Ops:
  8.0 0.0 copy-start
  8.0 0.9 copy.37
  8.9 0.1 convert_reduce_fusion
  9.0 0.1 fusion.13
  9.1 0.2 select_reduce_fusion.3
  9.3 0.1 fusion.10
  9.5 1.0 convolution_convert_fusion.5
  10.5 0.1 copy.40
  10.6 0.1 broadcast_in_dim.4
  10.7 82.5 %all_to_all.21 = bf16[32,7,2560]{2,1,0:T(8,128)(2,1)} all-to-all(bf16[32,7,2560]{2,1,0:T(8,128)(2,1)S(1)} %bitcast.58), channel_id=1, replica_groups=mesh['dp'=16,'expert'=32] {'expert'}, dimensions={0} | all-to-all | bytes 2293760 | tf_op jit(solution)/shard_map/all_to_all | solution.py:73
  93.2 1.5 reshape.115
  94.7 0.0 copy-start.3
  94.7 1.9 fusion.22
  96.6 1.2 multiply_convert_fusion.3
  97.8 1.6 convolution_convert_fusion.3
  99.4 2.3 reshape.116
  101.7 8.7 %all-to-all-start.1 = ((bf16[32,7,2560]{2,1,0:T(8,128)(2,1)}), bf16[32,7,2560]{2,1,0:T(8,128)(2,1)}, u32[]{:S(2)}, u32[]{:S(2)}) async-start(bf16[32,7,2560]{2,1,0:T(8,128)(2,1)} %reshape.116), calls=%async_computation.1 | async-start | bytes 2621440 | tf_op jit(solution)/shard_map/all_to_all | solution.py:81
  110.4 0.0 reduce-scatter.4.cloned.1.call-start
  110.4 0.8 fusion.21
  111.2 0.7 broadcast_multiply_fusion
  112.0 36.9 %all-to-all-done.1 = bf16[32,7,2560]{2,1,0:T(8,128)(2,1)} async-done(((bf16[32,7,2560]{2,1,0:T(8,128)(2,1)}), bf16[32,7,2560]{2,1,0:T(8,128)(2,1)}, u32[]{:S(2)}, u32[]{:S(2)}) %all-to-all-start.1) | async-done | bytes 1146912 | tf_op jit(solution)/shard_map/all_to_all | solution.py:81
  148.9 1.6 bitcast_reduce_fusion.1
  150.5 1.1 multiply_reduce_fusion
  151.6 0.2 select_reduce_fusion.1
  151.8 0.5 copy-done.13
  152.4 0.6 fusion.19
  152.9 1.4 copy.51
  154.3 1.0 fusion.6
  155.4 0.6 copy-done.10
  156.0 0.1 multiply_convert_fusion
  156.1 0.1 copy.43
  156.2 0.1 broadcast_in_dim.5
  156.3 74.3 %all_to_all.22 = bf16[32,7,2560]{2,1,0:T(8,128)(2,1)} all-to-all(bf16[32,7,2560]{2,1,0:T(8,128)(2,1)S(1)} %bitcast.59), channel_id=1, replica_groups=mesh['dp'=16,'expert'=32] {'expert'}, dimensions={0} | all-to-all | bytes 2293760 | tf_op jit(solution)/shard_map/all_to_all | solution.py:107
  230.5 2.3 reshape.120
  232.9 1.9 convolution_convert_fusion
  234.8 0.5 multiply_convert_fusion.1
  235.3 0.6 convolution_convert_fusion.1
  235.9 0.6 convolution_convert_fusion.2
  236.4 2.1 pad_maximum_fusion
  238.5 6.3 copy.60
  244.8 0.0 reduce-scatter.4.cloned.1.call-update
  244.8 1.3 copy-done.1
  246.1 0.6 fusion.23
  246.7 0.7 copy-done.4
  247.4 0.6 fusion
  248.0 1.3 reshape.121
  249.3 28.4 %all-to-all-start.3 = ((bf16[32,7,2560]{2,1,0:T(8,128)(2,1)}), bf16[32,7,2560]{2,1,0:T(8,128)(2,1)S(1)}, u32[]{:S(2)}, u32[]{:S(2)}) async-start(bf16[32,7,2560]{2,1,0:T(8,128)(2,1)} %reshape.121), calls=%async_computation.3 | async-start | bytes 2621440 | tf_op jit(solution)/shard_map/all_to_all | solution.py:32
  277.7 0.0 all-reduce.2.cloned.1.call-start
  277.8 0.1 select_reduce_fusion
  277.9 0.9 convolution_bitcast_fusion
  278.8 0.0 all-reduce.2.cloned.1.call-update
  278.8 0.9 fusion.2
  279.8 56.8 %all-to-all-done.3 = bf16[32,7,2560]{2,1,0:T(8,128)(2,1)S(1)} async-done(((bf16[32,7,2560]{2,1,0:T(8,128)(2,1)}), bf16[32,7,2560]{2,1,0:T(8,128)(2,1)S(1)}, u32[]{:S(2)}, u32[]{:S(2)}) %all-to-all-start.3) | async-done | bytes 1146912 | tf_op jit(solution)/shard_map/all_to_all | solution.py:32
  336.5 0.3 bitcast_reduce_fusion
  336.8 0.3 convolution_bitcast_fusion.1
  337.1 0.8 fusion.3
  337.9 75.4 %reduce-scatter.4.cloned.1.call-done = bf16[160,768]{1,0:T(8,128)(2,1)} async-done(((bf16[2560,768]{1,0:T(8,128)(2,1)}), bf16[160,768]{1,0:T(8,128)(2,1)}) %reduce-scatter.4.cloned.1.call-update) | async-done | bytes 245776
  413.3 1.1 copy.61
  414.5 0.1 fusion.20
  414.5 0.8 copy.47
  415.3 0.8 copy.48
  416.1 0.8 copy.49
  416.8 385.5 %all-reduce.2.cloned.1.call-done = f32[2560,8]{0,1:T(8,128)} async-done(((f32[2560,8]{0,1:T(8,128)}), f32[2560,8]{0,1:T(8,128)}) %all-reduce.2.cloned.1.call-update) | async-done | bytes 81936 | tf_op jit(solution)/shard_map/psum | solution.py:102
  802.4 1.5 copy.78
  (34 shorter events, 0.2 us)
Async XLA Ops:
  8.0 89.8 %copy-start = (bf16[2560,256]{1,0:T(8,128)(2,1)S(1)}, bf16[2560,256]{1,0:T(8,128)(2,1)}, u32[]{:S(2)}) copy-start(bf16[2560,256]{1,0:T(8,128)(2,1)} %param.12) | copy-start | bytes 3932164
  94.7 1.9 copy-start.3
  96.6 1.2 copy-start.8
  101.7 8.8 %copy-start.5 = (bf16[8,2560]{1,0:T(8,128)(2,1)S(1)}, bf16[8,2560]{1,0:T(8,128)(2,1)}, u32[]{:S(2)}) copy-start(bf16[8,2560]{1,0:T(8,128)(2,1)} %param.7) | copy-start | bytes 122884
  101.7 8.8 %copy-start.6 = (f32[2560,8]{0,1:T(8,128)S(1)}, f32[2560,8]{0,1:T(8,128)}, u32[]{:S(2)}) copy-start(f32[2560,8]{0,1:T(8,128)} %param.9) | copy-start | bytes 245764
  101.7 47.2 %all-to-all-start.1 = ((bf16[32,7,2560]{2,1,0:T(8,128)(2,1)}), bf16[32,7,2560]{2,1,0:T(8,128)(2,1)}, u32[]{:S(2)}, u32[]{:S(2)}) async-start(bf16[32,7,2560]{2,1,0:T(8,128)(2,1)} %reshape.116), calls=%async_computation.1 | async-start | bytes 2621440 | tf_op jit(solution)/shard_map/all_to_all | solution.py:81
  110.4 303.0 %reduce-scatter.4.cloned.1.call-start = ((), (), s32[]{:S(2)}) async-start(), calls=%async_computation.6 | async-start | bytes 4177920
  148.9 2.8 copy-start.12
  151.8 0.5 copy-start.13
  155.4 0.6 copy-start.10
  232.9 1.9 copy-start.2
  232.9 2.0 copy-start.9
  232.9 2.0 copy-start.15
  244.8 1.3 copy-start.1
  246.1 1.3 copy-start.4
  249.3 28.5 %copy-start.14 = (f32[8]{0:T(128)S(1)}, f32[8]{0:T(128)}, u32[]{:S(2)}) copy-start(f32[8]{0:T(128)} %copy-done.13) | copy-start | bytes 100
  249.3 29.5 %copy-start.11 = (f32[8,1,8,7]{2,1,3,0:T(1,128)S(1)}, f32[8,1,8,7]{2,1,3,0:T(1,128)}, u32[]{:S(2)}) copy-start(f32[8,1,8,7]{2,1,3,0:T(1,128)} %copy-done.10) | copy-start | bytes 5380
  249.3 87.2 %all-to-all-start.3 = ((bf16[32,7,2560]{2,1,0:T(8,128)(2,1)}), bf16[32,7,2560]{2,1,0:T(8,128)(2,1)S(1)}, u32[]{:S(2)}, u32[]{:S(2)}) async-start(bf16[32,7,2560]{2,1,0:T(8,128)(2,1)} %reshape.121), calls=%async_computation.3 | async-start | bytes 2621440 | tf_op jit(solution)/shard_map/all_to_all | solution.py:32
  277.7 524.7 %all-reduce.2.cloned.1.call-start = ((), (), s32[]{:S(2)}) async-start(), calls=%async_computation.5 | async-start | bytes 163840 | tf_op jit(solution)/shard_map/psum | solution.py:102
  277.9 59.2 %copy-start.7 = (f32[2560,8]{0,1:T(8,128)S(1)}, f32[2560,8]{0,1:T(8,128)}, u32[]{:S(2)}) copy-start(f32[2560,8]{0,1:T(8,128)} %param.9) | copy-start | bytes 245764
Sparse Core Ops, SparseCore 0:
  244.9 168.3 reduce-scatter.3
Sparse Core Ops, SparseCore 1:
  284.2 518.1 all-reduce.1
where the time goes:
time: 812 us; the launch traced here: 811 us
  waiting for transfers between devices  555 us (68%)
  blocking collectives  157 us (19%)
  starting transfers between devices  37.2 us (5%)
  local copies, waits for them, and re-layouts  24.5 us (3%)
  matrix products  16.2 us (2%)
  between operations  15.8 us (2%)
    psum x1, waiting for transfers between devices, local(): grad_router = lax.psum(router_part, ('dp', 'expert'))  386 us
    all_to_all x1, blocking collectives, local(): lax.all_to_all(outgoing_all, 'expert', split_axis=0, concat_axis=0, tiled...  82.5 us
    unnamed x3, waiting for transfers between devices  75.4 us
    all_to_all x1, blocking collectives, local(): lax.all_to_all(grad_outgoing_all, 'expert', split_axis=0, concat_axis=0,...  74.3 us
    all_to_all x1, waiting for transfers between devices, return_grads(): lax.all_to_all(input_part, 'expert', split_axis=0, concat_axis=0, tiled=T...  56.8 us
    all_to_all x1, waiting for transfers between devices, local(): lax.all_to_all(output, 'expert', split_axis=0, concat_axis=0, tiled=True)  36.9 us
    all_to_all x1, starting transfers between devices, return_grads(): lax.all_to_all(input_part, 'expert', split_axis=0, concat_axis=0, tiled=T...  28.4 us
  transfers between devices with their start and end apart: 4, of which 4 were waited for; matrix products, arithmetic and copies ran while one was open for 1% of the time, Pallas kernels for 0%

commit v1 on v0

--- a/solution.py
+++ b/solution.py
@@ -99,7 +99,7 @@
     logit_grad = (gate_pull - mean_pull) / denominator * affinity * (1.0 - affinity)
     per_logit = jnp.sum(choose_f * logit_grad[:, :, None], axis=1)
     router_part = jnp.dot(tokens_wide.T, per_logit, precision=highest)
-    grad_router = lax.psum(router_part, ("dp", "expert"))
+    grad_router = jnp.sum(lax.all_gather(router_part, ("dp", "expert")), axis=0)
     slot_gate = jnp.sum(gate_table, axis=0)
     grad_outgoing = (slot_gate[:, :, None] * grad_slots.astype(jnp.float32)).astype(jnp.bfloat16)
     grad_outgoing_all = jnp.repeat(grad_outgoing, sharing, axis=0)

time: 812 us -> 1240 us (1.53)
  waiting for transfers between devices: 555 us -> 964 us
  other arithmetic: 6.26 us -> 22.9 us
    all_gather x0 -> x1, waiting for transfers between devices: none -> 781 us  [local(): grad_router = jnp.sum(lax.all_gather(router_part, ('dp', 'expert')), axis=0)]
    psum x1 -> x0, waiting for transfers between devices: 386 us -> none  [local(): grad_router = lax.psum(router_part, ('dp', 'expert'))]
    reduce_sum x0 -> x1, other arithmetic: none -> 16.6 us  [local(): grad_router = jnp.sum(lax.all_gather(router_part, ('dp', 'expert')), axis=0)]
where the time goes in v1:
time: 1240 us
  waiting for transfers between devices  964 us (78%)
  blocking collectives  157 us (13%)
  starting transfers between devices  38.5 us (3%)
  other arithmetic  22.9 us (2%)
  local copies, waits for them, and re-layouts  22.3 us (2%)
  matrix products  16.2 us (1%)
  between operations  15.8 us (1%)
    all_gather x1, waiting for transfers between devices, local(): grad_router = jnp.sum(lax.all_gather(router_part, ('dp', 'expert')), axis=0)  781 us
    all_to_all x1, blocking collectives, local(): lax.all_to_all(outgoing_all, 'expert', split_axis=0, concat_axis=0, tiled...  82.4 us
    unnamed x3, waiting for transfers between devices  78.5 us
    all_to_all x1, blocking collectives, local(): lax.all_to_all(grad_outgoing_all, 'expert', split_axis=0, concat_axis=0,...  74.7 us
    all_to_all x1, waiting for transfers between devices, return_grads(): lax.all_to_all(input_part, 'expert', split_axis=0, concat_axis=0, tiled=T...  68.9 us
    all_to_all x1, waiting for transfers between devices, local(): lax.all_to_all(output, 'expert', split_axis=0, concat_axis=0, tiled=True)  36.5 us
    all_to_all x1, starting transfers between devices, return_grads(): lax.all_to_all(input_part, 'expert', split_axis=0, concat_axis=0, tiled=T...  29.8 us
  transfers between devices with their start and end apart: 4, of which 4 were waited for; matrix products, arithmetic and copies ran while one was open for 1% of the time, Pallas kernels for 0%

profile of v1, /device:TPU:1, one launch (start us, length us, event | category | flops | bytes accessed | tf_op | source)
XLA Modules:
  0.0 1237.4 jit_solution(2930279962897470249)
XLA Ops:
  8.0 0.0 copy-start
  8.0 0.9 copy.37
  8.9 0.1 convert_reduce_fusion
  9.0 0.1 fusion.13
  9.1 0.2 select_reduce_fusion.3
  9.3 0.1 fusion.10
  9.5 1.0 convolution_convert_fusion.5
  10.5 0.1 copy.40
  10.6 0.1 broadcast_in_dim.4
  10.7 82.4 %all_to_all.21 = bf16[32,7,2560]{2,1,0:T(8,128)(2,1)} all-to-all(bf16[32,7,2560]{2,1,0:T(8,128)(2,1)S(1)} %bitcast.60), channel_id=1, replica_groups=mesh['dp'=16,'expert'=32] {'expert'}, dimensions={0} | all-to-all | bytes 2293760 | tf_op jit(solution)/shard_map/all_to_all | solution.py:73
  93.1 1.5 reshape.115
  94.7 1.9 fusion.22
  96.6 1.2 multiply_convert_fusion.3
  97.7 1.6 convolution_convert_fusion.3
  99.3 2.3 reshape.116
  101.6 8.6 all-to-all-start.1
  110.3 0.0 reduce-scatter.4.cloned.1.call-start
  110.3 0.8 fusion.21
  111.1 0.7 broadcast_multiply_fusion
  111.9 36.5 %all-to-all-done.1 = bf16[32,7,2560]{2,1,0:T(8,128)(2,1)} async-done(((bf16[32,7,2560]{2,1,0:T(8,128)(2,1)}), bf16[32,7,2560]{2,1,0:T(8,128)(2,1)}, u32[]{:S(2)}, u32[]{:S(2)}) %all-to-all-start.1) | async-done | bytes 1146912 | tf_op jit(solution)/shard_map/all_to_all | solution.py:81
  148.4 1.6 bitcast_reduce_fusion.1
  150.0 1.1 multiply_reduce_fusion
  151.1 0.2 select_reduce_fusion.1
  151.3 0.5 copy-done.14
  151.8 0.6 fusion.19
  152.4 1.4 copy.51
  153.8 1.0 fusion.6
  154.8 0.0 copy-start.11
  154.9 0.6 copy-done.11
  155.4 0.1 multiply_convert_fusion
  155.6 0.1 copy.43
  155.7 0.1 broadcast_in_dim.5
  155.8 74.7 %all_to_all.22 = bf16[32,7,2560]{2,1,0:T(8,128)(2,1)} all-to-all(bf16[32,7,2560]{2,1,0:T(8,128)(2,1)S(1)} %bitcast.61), channel_id=1, replica_groups=mesh['dp'=16,'expert'=32] {'expert'}, dimensions={0} | all-to-all | bytes 2293760 | tf_op jit(solution)/shard_map/all_to_all | solution.py:107
  230.5 2.3 reshape.120
  232.8 1.9 convolution_convert_fusion
  234.8 0.5 multiply_convert_fusion.1
  235.3 0.6 convolution_convert_fusion.1
  235.8 0.6 convolution_convert_fusion.2
  236.4 2.1 pad_maximum_fusion
  238.5 6.3 copy.60
  244.8 0.0 reduce-scatter.4.cloned.1.call-update
  244.8 0.0 all-gather.3.cloned.1.call-start
  244.8 0.6 copy-done.15
  245.5 0.1 select_reduce_fusion
  245.6 0.9 convolution_bitcast_fusion
  246.4 0.0 all-gather.3.cloned.1.call-update
  246.5 0.6 fusion.23
  247.0 0.7 copy-done.5
  247.8 0.6 fusion
  248.4 1.3 reshape.121
  249.6 29.8 %all-to-all-start.3 = ((bf16[32,7,2560]{2,1,0:T(8,128)(2,1)}), bf16[32,7,2560]{2,1,0:T(8,128)(2,1)S(1)}, u32[]{:S(2)}, u32[]{:S(2)}) async-start(bf16[32,7,2560]{2,1,0:T(8,128)(2,1)} %reshape.121), calls=%async_computation.3 | async-start | bytes 2621440 | tf_op jit(solution)/shard_map/all_to_all | solution.py:32
  279.5 0.9 fusion.2
  280.4 68.9 %all-to-all-done.3 = bf16[32,7,2560]{2,1,0:T(8,128)(2,1)S(1)} async-done(((bf16[32,7,2560]{2,1,0:T(8,128)(2,1)}), bf16[32,7,2560]{2,1,0:T(8,128)(2,1)S(1)}, u32[]{:S(2)}, u32[]{:S(2)}) %all-to-all-start.3) | async-done | bytes 1146912 | tf_op jit(solution)/shard_map/all_to_all | solution.py:32
  349.3 0.3 bitcast_reduce_fusion
  349.6 0.3 convolution_bitcast_fusion.1
  349.9 0.8 fusion.3
  350.7 78.5 %reduce-scatter.4.cloned.1.call-done = bf16[160,768]{1,0:T(8,128)(2,1)} async-done(((bf16[2560,768]{1,0:T(8,128)(2,1)}), bf16[160,768]{1,0:T(8,128)(2,1)}) %reduce-scatter.4.cloned.1.call-update) | async-done | bytes 245776
  429.2 1.1 copy.61
  430.3 0.1 fusion.20
  430.4 0.8 copy.47
  431.2 0.8 copy.48
  431.9 0.8 copy.49
  432.7 780.6 %all-gather.3.cloned.1.call-done = f32[1310720,8]{0,1:T(8,128)} async-done(((f32[2560,8]{0,1:T(8,128)}), f32[1310720,8]{0,1:T(8,128)}) %all-gather.3.cloned.1.call-update) | async-done | bytes 41943056 | tf_op jit(solution)/shard_map/all_gather | solution.py:102
  1213.3 16.6 %reduce_sum.129 = f32[2560,8]{0,1:T(8,128)} reduce(f32[512,2560,8]{1,2,0:T(8,128)} %bitcast.59, f32[]{:T(128)} %constant.16.clone.1), dimensions={0}, to_apply=%region_13.14 | reduce | flops 10465280 | bytes 42024964 | tf_op jit(solution)/shard_map/reduce_sum | solution.py:102
  (36 shorter events, 0.2 us)
Async XLA Ops:
  8.0 89.7 %copy-start = (bf16[2560,256]{1,0:T(8,128)(2,1)S(1)}, bf16[2560,256]{1,0:T(8,128)(2,1)}, u32[]{:S(2)}) copy-start(bf16[2560,256]{1,0:T(8,128)(2,1)} %param.12) | copy-start | bytes 3932164
  94.7 1.9 copy-start.4
  96.6 1.2 copy-start.9
  101.6 8.7 copy-start.6
  101.6 8.7 copy-start.7
  101.6 46.7 %all-to-all-start.1 = ((bf16[32,7,2560]{2,1,0:T(8,128)(2,1)}), bf16[32,7,2560]{2,1,0:T(8,128)(2,1)}, u32[]{:S(2)}, u32[]{:S(2)}) async-start(bf16[32,7,2560]{2,1,0:T(8,128)(2,1)} %reshape.116), calls=%async_computation.1 | async-start | bytes 2621440 | tf_op jit(solution)/shard_map/all_to_all | solution.py:81
  110.3 318.9 %reduce-scatter.4.cloned.1.call-start = ((), (), s32[]{:S(2)}) async-start(), calls=%async_computation.6 | async-start | bytes 4177920
  148.4 2.8 copy-start.13
  151.3 0.5 copy-start.14
  154.8 0.6 copy-start.11
  232.8 2.0 copy-start.3
  232.8 2.0 copy-start.10
  232.8 2.0 copy-start.16
  244.8 0.7 copy-start.15
  244.8 1.7 copy-start.2
  244.8 968.5 %all-gather.3.cloned.1.call-start = ((), (), s32[]{:S(2)}) async-start(), calls=%async_computation.5 | async-start | bytes 42024960 | tf_op jit(solution)/shard_map/all_gather | solution.py:102
  246.5 1.3 copy-start.5
  249.6 29.8 %copy-start.12 = (f32[8,1,8,7]{2,1,3,0:T(1,128)S(1)}, f32[8,1,8,7]{2,1,3,0:T(1,128)}, u32[]{:S(2)}) copy-start(f32[8,1,8,7]{2,1,3,0:T(1,128)} %copy-done.11) | copy-start | bytes 5380
  249.6 99.7 %all-to-all-start.3 = ((bf16[32,7,2560]{2,1,0:T(8,128)(2,1)}), bf16[32,7,2560]{2,1,0:T(8,128)(2,1)S(1)}, u32[]{:S(2)}, u32[]{:S(2)}) async-start(bf16[32,7,2560]{2,1,0:T(8,128)(2,1)} %reshape.121), calls=%async_computation.3 | async-start | bytes 2621440 | tf_op jit(solution)/shard_map/all_to_all | solution.py:32
  279.5 70.4 %copy-start.8 = (f32[2560,8]{0,1:T(8,128)S(1)}, f32[2560,8]{0,1:T(8,128)}, u32[]{:S(2)}) copy-start(f32[2560,8]{0,1:T(8,128)} %param.9) | copy-start | bytes 245764
  1213.3 16.6 %copy-start.1 = (bf16[2560,256]{1,0:T(8,128)(2,1)S(1)}, bf16[2560,256]{1,0:T(8,128)(2,1)}, u32[]{:S(2)}) copy-start(bf16[2560,256]{1,0:T(8,128)(2,1)} %param.12) | copy-start | bytes 3932164
Sparse Core Ops, SparseCore 0:
  244.9 184.2 reduce-scatter.3
Sparse Core Ops, SparseCore 1:
  248.1 965.2 all-gather.2
